TPU v7x, 512 devices: a whole 4x4x16 slice. The times are simulated.
512 devices in a mesh: group: 16 (over z), shard: 32 (over y, x, core).
Axes of the slice: x: 4, y: 4, z: 16, core: 2. Of those that a mesh axis runs over, the one named last changes fastest.
Arguments:
- hot_row: int32 [4096, 39], P(('group', 'shard')), may hold values from 0 to 2047
- cold_row: int32 [4096, 39], P(('group', 'shard')), may hold values from 0 to 4095
- cold_owner: int32 [4096, 39], P(('group', 'shard')), may hold values from 0 to 31, as said below
- is_cold: int32 [4096, 39], P(('group', 'shard')), may hold values from 0 to 1
- grad_logit: float32 [4096], P(('group', 'shard')), may hold values from -12 to 12
- hot_table: bfloat16 [2048, 128], replicated, may hold values from -6 to 6
- cold_table: bfloat16 [131072, 128], P('shard'), may hold values from -6 to 6
- first_weight: bfloat16 [100, 1521], replicated, may hold values from -0.15625 to 0.15625
- second_weight: bfloat16 [100, 3900], replicated, may hold values from -0.09375 to 0.09375
- third_weight: bfloat16 [100, 3900], replicated, may hold values from -0.09375 to 0.09375
- out_weight: float32 [3, 100], replicated, may hold values from -0.375 to 0.375
Outputs:
- hot_grad: bfloat16 [2048, 128], replicated
- cold_grad: bfloat16 [131072, 128], P('shard')
- logits: float32 [4096], P(('group', 'shard'))
Inputs may be any that keep to these rules, and one draw needn't show every extreme that they name: `cold_owner`: among the 312 lookups of one device, at most 9 with is_cold 1 name the same owner; for each index of group, one owner receives exactly 9 such lookups from every device of that group index.
All inputs are finite; a program needn't handle non-finite values.
Results may differ from a plain program's by a relative error of at most 0.014.
Values may be sent and summed in bfloat16 or wider, within the bound.
No kernel may reach another device: no remote copies, remote signals or barrier semaphores. Data moves between devices by JAX's collectives and lax.ppermute only.
A program may use at most 64 MiB of HBM per device.

v0:
```python
import jax
import jax.numpy as jnp
from jax import lax
from jax.sharding import PartitionSpec as P


def sample_pass(embedded, grad_logit, layer_weights, out_weight):
    batch_rows, fields, breadth = embedded.shape
    base_wide = embedded.astype(jnp.float32)
    previous = embedded
    layer_inputs = []
    logit_sum = jnp.zeros((batch_rows,), jnp.float32)
    for section_index in range(len(layer_weights)):
        weight = layer_weights[section_index]
        below_maps = previous.shape[1]
        outer_rows = (
            previous.astype(jnp.float32)[:, :, None, :] * base_wide[:, None, :, :]
        ).astype(jnp.bfloat16)
        outer_rows = outer_rows.reshape(batch_rows, below_maps * fields, breadth)
        current = jnp.einsum(
            "hk,bke->bhe", weight, outer_rows, preferred_element_type=jnp.float32
        ).astype(jnp.bfloat16)
        pooled = jnp.sum(current.astype(jnp.float32), axis=2)
        logit_sum = logit_sum + jnp.sum(pooled * out_weight[section_index][None, :], axis=1)
        layer_inputs.append(previous)
        previous = current
    grad_embedded = jnp.zeros((batch_rows, fields, breadth), jnp.float32)
    carried = jnp.zeros((batch_rows, out_weight.shape[1], breadth), jnp.float32)
    for section_index in reversed(range(len(layer_weights))):
        weight = layer_weights[section_index]
        lower_state = layer_inputs[section_index]
        below_maps = lower_state.shape[1]
        grad_state = carried + grad_logit[:, None, None] * out_weight[section_index][None, :, None]
        grad_low = grad_state.astype(jnp.bfloat16)
        grad_outer = jnp.einsum("hk,bhe->bke", weight, grad_low, preferred_element_type=jnp.float32)
        grad_outer = grad_outer.reshape(batch_rows, below_maps, fields, breadth)
        grad_embedded = grad_embedded + jnp.sum(
            grad_outer * lower_state.astype(jnp.float32)[:, :, None, :], axis=1
        )
        carried = jnp.sum(grad_outer * base_wide[:, None, :, :], axis=2)
    grad_embedded = grad_embedded + carried
    return (logit_sum, grad_embedded)


def local(
    hot_row,
    cold_row,
    cold_owner,
    is_cold,
    grad_logit,
    hot_table,
    cold_table,
    first_weight,
    second_weight,
    third_weight,
    out_weight,
):
    samples, fields = hot_row.shape
    breadth = hot_table.shape[1]
    owners = lax.axis_size("shard")
    lookups = samples * fields
    capacity = lookups // owners
    owner_flat = cold_owner.reshape(lookups)
    cold_flag = is_cold.reshape(lookups) == 1
    wanted = jnp.logical_and(
        owner_flat[:, None] == jnp.arange(owners, dtype=jnp.int32)[None, :], cold_flag[:, None]
    ).astype(jnp.int32)
    earlier = jnp.cumsum(wanted, axis=0) - wanted
    position = jnp.sum(earlier * wanted, axis=1)
    target = jnp.where(cold_flag, owner_flat * capacity + position, owners * capacity)
    asked_rows = jnp.where(cold_flag, cold_row.reshape(lookups), -1)
    request = jnp.full((owners * capacity + 1,), -1, jnp.int32).at[target].set(asked_rows)
    request = request[: owners * capacity].reshape(owners, capacity)
    requested = lax.all_to_all(request, "shard", split_axis=0, concat_axis=0, tiled=True)
    present = requested >= 0
    table_rows = jnp.take(cold_table, jnp.maximum(requested, 0), axis=0)
    table_rows = jnp.where(present[:, :, None], table_rows, jnp.zeros_like(table_rows))
    returned = lax.all_to_all(table_rows, "shard", split_axis=0, concat_axis=0, tiled=True)
    fetched_flat = jnp.concatenate(
        [returned.reshape(owners * capacity, breadth), jnp.zeros((1, breadth), jnp.bfloat16)],
        axis=0,
    )
    cold_values = jnp.take(fetched_flat, target, axis=0)
    hot_values = jnp.take(hot_table, hot_row.reshape(lookups), axis=0)
    embedded = jnp.where(cold_flag[:, None], cold_values, hot_values).reshape(
        samples, fields, breadth
    )
    layer_weights = (first_weight, second_weight, third_weight)

    def one_sample(sample_pair):
        logit_one, grad_one = sample_pass(
            sample_pair[0][None], sample_pair[1][None], layer_weights, out_weight
        )
        return (logit_one[0], grad_one[0])

    logits, gradients = lax.map(one_sample, (embedded, grad_logit))
    gradients = gradients.reshape(lookups, breadth)
    cold_terms = jnp.where(cold_flag[:, None], gradients, 0.0)
    hot_terms = jnp.where(cold_flag[:, None], 0.0, gradients)
    outgoing = jnp.zeros((owners * capacity + 1, breadth), jnp.float32).at[target].add(cold_terms)
    outgoing = outgoing[: owners * capacity].reshape(owners, capacity, breadth)
    incoming = lax.all_to_all(
        outgoing.astype(jnp.bfloat16), "shard", split_axis=0, concat_axis=0, tiled=True
    ).astype(outgoing.dtype)
    shard_rows = cold_table.shape[0]
    safe_ids = jnp.maximum(requested, 0)
    cold_local = jax.ops.segment_sum(
        incoming.reshape(-1, breadth), safe_ids.reshape(-1), num_segments=shard_rows
    )
    cold_total = lax.psum(cold_local.astype(jnp.bfloat16), "group")
    hot_local = jax.ops.segment_sum(
        hot_terms, hot_row.reshape(lookups), num_segments=hot_table.shape[0]
    )
    hot_grad = lax.psum(hot_local, ("group", "shard")).astype(jnp.bfloat16)
    return (hot_grad, cold_total, logits)


def solution(mesh):
    return jax.shard_map(
        local,
        mesh=mesh,
        in_specs=(
            P(("group", "shard"), None),
            P(("group", "shard"), None),
            P(("group", "shard"), None),
            P(("group", "shard"), None),
            P(("group", "shard")),
            P(),
            P("shard", None),
            P(),
            P(),
            P(),
            P(),
        ),
        out_specs=(P(), P("shard", None), P(("group", "shard"))),
        check_vma=False,
    )
```

profile of v0, /device:TPU:2, one launch (start us, length us, event | category | flops | bytes accessed | tf_op | source)
XLA Modules:
  0.0 380.4 jit_solution(5741558667474088209)
XLA Ops:
  11.8 2.9 scatter_custom_fusion
  15.4 9.4 %all-to-all-start = ((s32[32,1,9]{2,1,0:T(1,128)}), s32[32,1,9]{2,1,0:T(1,128)S(1)}, u32[]{:S(2)}, u32[]{:S(2)}) async-start(s32[32,1,9]{2,1,0:T(1,128)} %bitcast.28), calls=%async_computation | async-start | bytes 32768 | tf_op jit(solution)/shard_map/all_to_all | solution.py:74
  26.5 2.3 gather_fusion.2
  28.8 2.2 all-to-all-done
  31.3 1.4 gather_fusion
  33.8 5.3 %all-to-all-start.1 = ((bf16[32,9,128]{2,1,0:T(8,128)(2,1)}), bf16[32,9,128]{2,1,0:T(8,128)(2,1)S(1)}, u32[]{:S(2)}, u32[]{:S(2)}) async-start(bf16[32,9,128]{2,1,0:T(8,128)(2,1)} %select_select_fusion), calls=%async_computation.1 | async-start | bytes 262144 | tf_op jit(solution)/shard_map/all_to_all | solution.py:78
  39.2 6.5 %all-to-all-done.1 = bf16[32,9,128]{2,1,0:T(8,128)(2,1)S(1)} async-done(((bf16[32,9,128]{2,1,0:T(8,128)(2,1)}), bf16[32,9,128]{2,1,0:T(8,128)(2,1)S(1)}, u32[]{:S(2)}, u32[]{:S(2)}) %all-to-all-start.1) | async-done | bytes 73760 | tf_op jit(solution)/shard_map/all_to_all | solution.py:78
  45.8 1.4 gather_fusion.1
  48.1 165.5 %while.12 = (s32[]{:T(128)}, f32[8]{0:T(128)}, f32[8,39,128]{2,1,0:T(8,128)}, bf16[8,39,128]{2,1,0:T(8,128)(2,1)}, bf16[100,1521]{1,0:T(8,128)(2,1)S(1)}, /*inde...) while((s32[]{:T(128)}, f32[8]{0:T(128)}, ...), condition=%wide.region_17.18_spmd, body=%wide.region_4.17_spmd.sunk | while | flops 484535232 | bytes 39531044 | solution.py:96
  49.8 1.6 fusion.65
  52.0 1.7 fusion.66
  56.3 1.8 convolution_bitcast_fusion.6
  58.2 1.6 reshape.545
  60.9 1.8 convolution_bitcast_fusion.7
  62.8 1.6 reshape.546
  70.5 1.6 fusion.65
  72.7 1.7 fusion.66
  77.0 1.8 convolution_bitcast_fusion.6
  78.9 1.6 reshape.545
  81.6 1.8 convolution_bitcast_fusion.7
  83.5 1.6 reshape.546
  91.2 1.6 fusion.65
  93.3 1.7 fusion.66
  97.7 1.8 convolution_bitcast_fusion.6
  99.6 1.6 reshape.545
  102.3 1.8 convolution_bitcast_fusion.7
  104.1 1.6 reshape.546
  111.9 1.6 fusion.65
  114.0 1.7 fusion.66
  118.4 1.8 convolution_bitcast_fusion.6
  120.2 1.6 reshape.545
  123.0 1.8 convolution_bitcast_fusion.7
  124.8 1.6 reshape.546
  132.6 1.6 fusion.65
  134.7 1.7 fusion.66
  139.1 1.8 convolution_bitcast_fusion.6
  140.9 1.6 reshape.545
  143.7 1.8 convolution_bitcast_fusion.7
  145.5 1.6 reshape.546
  153.2 1.6 fusion.65
  155.4 1.7 fusion.66
  159.7 1.8 convolution_bitcast_fusion.6
  161.6 1.6 reshape.545
  164.3 1.8 convolution_bitcast_fusion.7
  166.2 1.6 reshape.546
  173.9 1.6 fusion.65
  176.1 1.7 fusion.66
  180.4 1.8 convolution_bitcast_fusion.6
  182.3 1.6 reshape.545
  185.0 1.8 convolution_bitcast_fusion.7
  186.9 1.6 reshape.546
  194.6 1.6 fusion.65
  196.8 1.7 fusion.66
  201.1 1.8 convolution_bitcast_fusion.6
  203.0 1.6 reshape.545
  205.7 1.8 convolution_bitcast_fusion.7
  207.5 1.6 reshape.546
  214.5 2.0 scatter_custom_fusion.2
  216.6 11.5 %all_to_all.19 = bf16[32,9,128]{2,1,0:T(8,128)(2,1)S(1)} all-to-all(bf16[32,9,128]{2,1,0:T(8,128)(2,1)S(1)} %convert_element_type.112), channel_id=1, replica_groups=mesh['group'=16,'shard'=32] {'shard'}, dimensions={0} | all-to-all | bytes 147456 | tf_op jit(solution)/shard_map/all_to_all | solution.py:102
  228.2 2.5 scatter_custom_fusion.3
  231.9 2.0 scatter_custom_fusion.1
  233.9 110.9 %all-reduce.6 = bf16[2048,128]{1,0:T(8,128)(2,1)} all-reduce(f32[2048,128]{1,0:T(8,128)S(1)} %scatter_custom_fusion.1), channel_id=1, replica_groups=mesh['group'=16,'shard'=32] {'group','shard'}, use_global_device_ids=true, to_apply=%region_19.20 | all-reduce | flops 262144 | bytes 1572864 | tf_op jit(solution)/shard_map/psum | solution.py:114
  344.8 26.5 %all-reduce.5.cloned.1.call-done = bf16[4096,128]{1,0:T(8,128)(2,1)} async-done(((bf16[4096,128]{1,0:T(8,128)(2,1)}), bf16[4096,128]{1,0:T(8,128)(2,1)}) %all-reduce.5.cloned.1.call-update) | async-done | bytes 1048592 | tf_op jit(solution)/shard_map/psum | solution.py:110
  371.3 2.3 copy.47
  (280 shorter events, 80.0 us)
Async XLA Ops:
  7.2 24.2 %copy-start = (bf16[4096,128]{1,0:T(8,128)(2,1)S(1)}, bf16[4096,128]{1,0:T(8,128)(2,1)}, u32[]{:S(2)}) copy-start(bf16[4096,128]{1,0:T(8,128)(2,1)} %param.19) | copy-start | bytes 3145732
  8.0 23.3 %copy-start.7 = (pred[312]{0:T(512)(128)(4,1)}, pred[312]{0:T(512)(128)(4,1)S(1)}, u32[]{:S(2)}) copy-start(pred[312]{0:T(512)(128)(4,1)S(1)} %eq.48) | copy-start | bytes 940
  11.8 35.4 %copy-start.9 = (s32[312]{0:T(512)}, s32[312]{0:T(512)S(1)}, u32[]{:S(2)}) copy-start(s32[312]{0:T(512)S(1)} %fusion.26) | copy-start | bytes 3748
  15.4 15.6 %all-to-all-start = ((s32[32,1,9]{2,1,0:T(1,128)}), s32[32,1,9]{2,1,0:T(1,128)S(1)}, u32[]{:S(2)}, u32[]{:S(2)}) async-start(s32[32,1,9]{2,1,0:T(1,128)} %bitcast.28), calls=%async_computation | async-start | bytes 32768 | tf_op jit(solution)/shard_map/all_to_all | solution.py:74
  26.4 21.7 %copy-start.3 = (bf16[100,1521]{1,0:T(8,128)(2,1)S(1)}, bf16[100,1521]{1,0:T(8,128)(2,1)}, u32[]{:S(2)}) copy-start(bf16[100,1521]{1,0:T(8,128)(2,1)} %param.20) | copy-start | bytes 912604
  26.4 21.6 %copy-start.6 = (f32[3,100]{1,0:T(4,128)S(1)}, f32[3,100]{1,0:T(4,128)}, u32[]{:S(2)}) copy-start(f32[3,100]{1,0:T(4,128)} %param.23) | copy-start | bytes 3604
  31.3 7.8 %copy-start.10 = (s32[288]{0:T(512)}, s32[288]{0:T(512)S(1)}, u32[]{:S(2)}) copy-start(s32[288]{0:T(512)S(1)} %reshape.473) | copy-start | bytes 3460
  33.8 11.9 %all-to-all-start.1 = ((bf16[32,9,128]{2,1,0:T(8,128)(2,1)}), bf16[32,9,128]{2,1,0:T(8,128)(2,1)S(1)}, u32[]{:S(2)}, u32[]{:S(2)}) async-start(bf16[32,9,128]{2,1,0:T(8,128)(2,1)} %select_select_fusion), calls=%async_computation.1 | async-start | bytes 262144 | tf_op jit(solution)/shard_map/all_to_all | solution.py:78
  39.1 332.2 %all-reduce.5.cloned.1.call-start = ((), (), s32[]{:S(2)}) async-start(), calls=%async_computation.3 | async-start | bytes 2097152 | tf_op jit(solution)/shard_map/psum | solution.py:110
  52.0 4.4 %copy-start.2 = (bf16[100,3900]{1,0:T(8,128)(2,1)S(1)}, bf16[100,3900]{1,0:T(8,128)(2,1)}, u32[]{:S(2)}) copy-start(bf16[100,3900]{1,0:T(8,128)(2,1)} %get-tuple-element.208) | copy-start | bytes 2340004 | tf_op jit(solution)/shard_map/while
  59.8 1.1 copy-start.1
  65.0 0.7 copy-start.4
  65.0 3.1 copy-start.11
  68.3 0.5 copy-start.12
  72.7 4.4 %copy-start.2 = (bf16[100,3900]{1,0:T(8,128)(2,1)S(1)}, bf16[100,3900]{1,0:T(8,128)(2,1)}, u32[]{:S(2)}) copy-start(bf16[100,3900]{1,0:T(8,128)(2,1)} %get-tuple-element.208) | copy-start | bytes 2340004 | tf_op jit(solution)/shard_map/while
  80.5 1.1 copy-start.1
  85.7 0.7 copy-start.4
  85.7 3.1 copy-start.11
  88.9 0.5 copy-start.12
  93.3 4.4 %copy-start.2 = (bf16[100,3900]{1,0:T(8,128)(2,1)S(1)}, bf16[100,3900]{1,0:T(8,128)(2,1)}, u32[]{:S(2)}) copy-start(bf16[100,3900]{1,0:T(8,128)(2,1)} %get-tuple-element.208) | copy-start | bytes 2340004 | tf_op jit(solution)/shard_map/while
  101.1 1.1 copy-start.1
  106.3 0.7 copy-start.4
  106.4 3.1 copy-start.11
  109.6 0.5 copy-start.12
  114.0 4.4 %copy-start.2 = (bf16[100,3900]{1,0:T(8,128)(2,1)S(1)}, bf16[100,3900]{1,0:T(8,128)(2,1)}, u32[]{:S(2)}) copy-start(bf16[100,3900]{1,0:T(8,128)(2,1)} %get-tuple-element.208) | copy-start | bytes 2340004 | tf_op jit(solution)/shard_map/while
  121.8 1.1 copy-start.1
  127.0 0.7 copy-start.4
  127.0 3.1 copy-start.11
  130.3 0.5 copy-start.12
  134.7 4.4 %copy-start.2 = (bf16[100,3900]{1,0:T(8,128)(2,1)S(1)}, bf16[100,3900]{1,0:T(8,128)(2,1)}, u32[]{:S(2)}) copy-start(bf16[100,3900]{1,0:T(8,128)(2,1)} %get-tuple-element.208) | copy-start | bytes 2340004 | tf_op jit(solution)/shard_map/while
  142.5 1.1 copy-start.1
  147.7 0.7 copy-start.4
  147.7 3.1 copy-start.11
  151.0 0.5 copy-start.12
  155.4 4.4 %copy-start.2 = (bf16[100,3900]{1,0:T(8,128)(2,1)S(1)}, bf16[100,3900]{1,0:T(8,128)(2,1)}, u32[]{:S(2)}) copy-start(bf16[100,3900]{1,0:T(8,128)(2,1)} %get-tuple-element.208) | copy-start | bytes 2340004 | tf_op jit(solution)/shard_map/while
  163.2 1.1 copy-start.1
  168.4 0.7 copy-start.4
  168.4 3.1 copy-start.11
  171.7 0.5 copy-start.12
  176.1 4.4 %copy-start.2 = (bf16[100,3900]{1,0:T(8,128)(2,1)S(1)}, bf16[100,3900]{1,0:T(8,128)(2,1)}, u32[]{:S(2)}) copy-start(bf16[100,3900]{1,0:T(8,128)(2,1)} %get-tuple-element.208) | copy-start | bytes 2340004 | tf_op jit(solution)/shard_map/while
  183.9 1.1 copy-start.1
  189.1 0.7 copy-start.4
  189.1 3.1 copy-start.11
  192.4 0.5 copy-start.12
  196.7 4.4 %copy-start.2 = (bf16[100,3900]{1,0:T(8,128)(2,1)S(1)}, bf16[100,3900]{1,0:T(8,128)(2,1)}, u32[]{:S(2)}) copy-start(bf16[100,3900]{1,0:T(8,128)(2,1)} %get-tuple-element.208) | copy-start | bytes 2340004 | tf_op jit(solution)/shard_map/while
  204.6 1.1 copy-start.1
  209.8 0.7 copy-start.4
  209.8 3.1 copy-start.11
  213.0 0.5 copy-start.12
  230.7 1.1 copy-start.5
  230.7 1.2 copy-start.8
Sparse Core Ops, SparseCore 0:
  231.9 139.3 all-reduce.4
where the time goes:
time: 383 us; the launch traced here: 380 us
  blocking collectives  122 us (32%)
  local copies, waits for them, and re-layouts  63.4 us (17%)
  matrix products  62.2 us (16%)
  other arithmetic  52.6 us (14%)
  waiting for transfers between devices  35.3 us (9%)
  loops' own time  15.5 us (4%)
  starting transfers between devices  14.7 us (4%)
  between operations  14.3 us (4%)
    psum x1, blocking collectives, local(): hot_grad = lax.psum(hot_local, ('group', 'shard')).astype(jnp.bfloat16)  111 us
    dot_general x24, matrix products, sample_pass(): jnp.einsum('hk,bhe->bke', weight, grad_low, preferred_element_type=jnp.fl...  33 us
    dot_general x24, matrix products, sample_pass(): jnp.einsum('hk,bke->bhe', weight, outer_rows, preferred_element_type=jnp....  29.2 us
    psum x1, waiting for transfers between devices, local(): cold_total = lax.psum(cold_local.astype(jnp.bfloat16), 'group')  26.5 us
    reshape x24, local copies, waits for them, and re-layouts, sample_pass(): grad_outer = grad_outer.reshape(batch_rows, below_maps, fields, breadth)  25.9 us
    another operation x1, loops' own time, local(): logits, gradients = lax.map(one_sample, (embedded, grad_logit))  15.5 us
    reduce_sum x24, other arithmetic, sample_pass(): jnp.sum(grad_outer * lower_state.astype(jnp.float32)[:, :, None, :], axis=1)  15.3 us
    all_to_all x1, blocking collectives, local(): lax.all_to_all(outgoing.astype(jnp.bfloat16), 'shard', split_axis=0, conc...  11.5 us
  transfers between devices with their start and end apart: 3, of which 3 were waited for; matrix products, arithmetic and copies ran while one was open for 2% of the time, Pallas kernels for 0%

commit v1 on v0

--- a/solution.py
+++ b/solution.py
@@ -2,6 +2,11 @@
 import jax.numpy as jnp
 from jax import lax
 from jax.sharding import PartitionSpec as P
+
+
+def by_each_axis(array, axis_one, axis_two):
+    inner = lax.psum(array, axis_one)
+    return lax.psum(inner, axis_two)
 
 
 def sample_pass(embedded, grad_logit, layer_weights, out_weight):
@@ -111,7 +116,7 @@
     hot_local = jax.ops.segment_sum(
         hot_terms, hot_row.reshape(lookups), num_segments=hot_table.shape[0]
     )
-    hot_grad = lax.psum(hot_local, ("group", "shard")).astype(jnp.bfloat16)
+    hot_grad = by_each_axis(hot_local, "shard", "group").astype(jnp.bfloat16)
     return (hot_grad, cold_total, logits)
 
 

time: 383 us -> 510 us (1.33)
  waiting for transfers between devices: 35.3 us -> 194 us
  blocking collectives: 122 us -> 86.4 us
    psum x0 -> x1, waiting for transfers between devices: none -> 118 us  [by_each_axis(): inner = lax.psum(array, axis_one)]
    psum x1, waiting for transfers between devices: 26.5 us -> 68.1 us  [local(): cold_total = lax.psum(cold_local.astype(jnp.bfloat16), 'group')]
    psum x1, blocking collectives: 111 us -> 75.1 us  [by_each_axis(): return lax.psum(inner, axis_two)]
  transfers between devices with their start and end apart: 3 -> 4, of which waited for: 3 -> 4; matrix products, arithmetic and copies ran while one was open for 2% -> 2% of each run, Pallas kernels for 0% -> 0%
where the time goes in v1:
time: 510 us; the launch traced here: 507 us
  waiting for transfers between devices  194 us (38%)
  blocking collectives  86.4 us (17%)
  local copies, waits for them, and re-layouts  64.6 us (13%)
  matrix products  62.3 us (12%)
  other arithmetic  53.5 us (10%)
  starting transfers between devices  16.1 us (3%)
  loops' own time  15.9 us (3%)
  between operations  14.3 us (3%)
    psum x1, waiting for transfers between devices, by_each_axis(): inner = lax.psum(array, axis_one)  118 us
    psum x1, blocking collectives, by_each_axis(): return lax.psum(inner, axis_two)  75.1 us
    psum x1, waiting for transfers between devices, local(): cold_total = lax.psum(cold_local.astype(jnp.bfloat16), 'group')  68.1 us
    dot_general x24, matrix products, sample_pass(): jnp.einsum('hk,bhe->bke', weight, grad_low, preferred_element_type=jnp.fl...  33 us
    dot_general x24, matrix products, sample_pass(): jnp.einsum('hk,bke->bhe', weight, outer_rows, preferred_element_type=jnp....  29.3 us
    reshape x24, local copies, waits for them, and re-layouts, sample_pass(): grad_outer = grad_outer.reshape(batch_rows, below_maps, fields, breadth)  25.9 us
    another operation x1, loops' own time, local(): logits, gradients = lax.map(one_sample, (embedded, grad_logit))  15.9 us
    reduce_sum x24, other arithmetic, sample_pass(): jnp.sum(grad_outer * lower_state.astype(jnp.float32)[:, :, None, :], axis=1)  15.3 us
  transfers between devices with their start and end apart: 4, of which 4 were waited for; matrix products, arithmetic and copies ran while one was open for 2% of the time, Pallas kernels for 0%

profile of v1, /device:TPU:2, one launch (start us, length us, event | category | flops | bytes accessed | tf_op | source)
XLA Modules:
  0.0 506.8 jit_solution(11954460398220408562)
XLA Ops:
  11.8 2.9 scatter_custom_fusion
  15.4 9.4 %all-to-all-start = ((s32[32,1,9]{2,1,0:T(1,128)}), s32[32,1,9]{2,1,0:T(1,128)S(1)}, u32[]{:S(2)}, u32[]{:S(2)}) async-start(s32[32,1,9]{2,1,0:T(1,128)} %bitcast.28), calls=%async_computation | async-start | bytes 32768 | tf_op jit(solution)/shard_map/all_to_all | solution.py:79
  27.8 2.3 gather_fusion.2
  31.3 1.4 gather_fusion
  33.8 6.6 %all-to-all-start.1 = ((bf16[32,9,128]{2,1,0:T(8,128)(2,1)}), bf16[32,9,128]{2,1,0:T(8,128)(2,1)S(1)}, u32[]{:S(2)}, u32[]{:S(2)}) async-start(bf16[32,9,128]{2,1,0:T(8,128)(2,1)} %select_select_fusion), calls=%async_computation.1 | async-start | bytes 262144 | tf_op jit(solution)/shard_map/all_to_all | solution.py:83
  40.5 6.5 %all-to-all-done.1 = bf16[32,9,128]{2,1,0:T(8,128)(2,1)S(1)} async-done(((bf16[32,9,128]{2,1,0:T(8,128)(2,1)}), bf16[32,9,128]{2,1,0:T(8,128)(2,1)S(1)}, u32[]{:S(2)}, u32[]{:S(2)}) %all-to-all-start.1) | async-done | bytes 73760 | tf_op jit(solution)/shard_map/all_to_all | solution.py:83
  47.1 1.4 gather_fusion.1
  49.4 165.9 %while.12 = (s32[]{:T(128)}, f32[8]{0:T(128)}, f32[8,39,128]{2,1,0:T(8,128)}, bf16[8,39,128]{2,1,0:T(8,128)(2,1)}, bf16[100,1521]{1,0:T(8,128)(2,1)S(1)}, /*inde...) while((s32[]{:T(128)}, f32[8]{0:T(128)}, ...), condition=%wide.region_17.18_spmd, body=%wide.region_4.17_spmd.sunk | while | flops 484535232 | bytes 39531044 | solution.py:101
  51.2 1.6 fusion.65
  53.3 1.7 fusion.66
  57.7 1.8 convolution_bitcast_fusion.6
  59.5 1.6 reshape.545
  62.3 1.8 convolution_bitcast_fusion.7
  64.1 1.6 reshape.546
  71.9 1.6 fusion.65
  74.1 1.7 fusion.66
  78.4 1.8 convolution_bitcast_fusion.6
  80.3 1.6 reshape.545
  83.0 1.8 convolution_bitcast_fusion.7
  84.9 1.6 reshape.546
  92.6 1.6 fusion.65
  94.8 1.7 fusion.66
  99.2 1.8 convolution_bitcast_fusion.6
  101.0 1.6 reshape.545
  103.7 1.8 convolution_bitcast_fusion.7
  105.6 1.6 reshape.546
  113.4 1.6 fusion.65
  115.5 1.7 fusion.66
  119.9 1.8 convolution_bitcast_fusion.6
  121.7 1.6 reshape.545
  124.5 1.8 convolution_bitcast_fusion.7
  126.3 1.6 reshape.546
  134.1 1.6 fusion.65
  136.3 1.7 fusion.66
  140.6 1.8 convolution_bitcast_fusion.6
  142.5 1.6 reshape.545
  145.2 1.8 convolution_bitcast_fusion.7
  147.1 1.6 reshape.546
  154.9 1.6 fusion.65
  157.0 1.7 fusion.66
  161.4 1.8 convolution_bitcast_fusion.6
  163.2 1.6 reshape.545
  166.0 1.8 convolution_bitcast_fusion.7
  167.8 1.6 reshape.546
  175.6 1.6 fusion.65
  177.8 1.7 fusion.66
  182.1 1.8 convolution_bitcast_fusion.6
  184.0 1.6 reshape.545
  186.7 1.8 convolution_bitcast_fusion.7
  188.6 1.6 reshape.546
  196.4 1.6 fusion.65
  198.5 1.7 fusion.66
  202.9 1.8 convolution_bitcast_fusion.6
  204.7 1.6 reshape.545
  207.5 1.8 convolution_bitcast_fusion.7
  209.3 1.6 reshape.546
  216.3 2.8 scatter_custom_fusion.1
  219.2 2.0 scatter_custom_fusion.2
  221.3 11.4 %all_to_all.19 = bf16[32,9,128]{2,1,0:T(8,128)(2,1)S(1)} all-to-all(bf16[32,9,128]{2,1,0:T(8,128)(2,1)S(1)} %convert_element_type.112), channel_id=1, replica_groups=mesh['group'=16,'shard'=32] {'shard'}, dimensions={0} | all-to-all | bytes 147456 | tf_op jit(solution)/shard_map/all_to_all | solution.py:107
  232.7 2.5 scatter_custom_fusion.3
  236.4 118.2 %all-reduce.6.cloned.1.call-done = f32[2048,128]{1,0:T(8,128)} async-done(((f32[2048,128]{1,0:T(8,128)}), f32[2048,128]{1,0:T(8,128)}) %all-reduce.6.cloned.1.call-update) | async-done | bytes 1048592 | tf_op jit(solution)/shard_map/psum | solution.py:8
  354.6 75.1 %all-reduce.9 = bf16[2048,128]{1,0:T(8,128)(2,1)} all-reduce(f32[2048,128]{1,0:T(8,128)} %all-reduce.6.cloned.1.call-done), channel_id=1, replica_groups=mesh['group'=16,'shard'=32] {'group'}, use_global_device_ids=true, to_apply=%region_20.21 | all-reduce | flops 262144 | bytes 1572864 | tf_op jit(solution)/shard_map/psum | solution.py:9
  429.7 68.1 %all-reduce.8.cloned.1.call-done = bf16[4096,128]{1,0:T(8,128)(2,1)} async-done(((bf16[4096,128]{1,0:T(8,128)(2,1)}), bf16[4096,128]{1,0:T(8,128)(2,1)}) %all-reduce.8.cloned.1.call-update) | async-done | bytes 1048592 | tf_op jit(solution)/shard_map/psum | solution.py:115
  497.7 2.3 copy.48
  (281 shorter events, 82.3 us)
Async XLA Ops:
  7.2 24.2 %copy-start = (bf16[4096,128]{1,0:T(8,128)(2,1)S(1)}, bf16[4096,128]{1,0:T(8,128)(2,1)}, u32[]{:S(2)}) copy-start(bf16[4096,128]{1,0:T(8,128)(2,1)} %param.19) | copy-start | bytes 3145732
  8.0 23.3 %copy-start.6 = (pred[312]{0:T(512)(128)(4,1)}, pred[312]{0:T(512)(128)(4,1)S(1)}, u32[]{:S(2)}) copy-start(pred[312]{0:T(512)(128)(4,1)S(1)} %eq.48) | copy-start | bytes 940
  11.8 36.7 %copy-start.8 = (s32[312]{0:T(512)}, s32[312]{0:T(512)S(1)}, u32[]{:S(2)}) copy-start(s32[312]{0:T(512)S(1)} %fusion.26) | copy-start | bytes 3748
  15.4 15.6 %all-to-all-start = ((s32[32,1,9]{2,1,0:T(1,128)}), s32[32,1,9]{2,1,0:T(1,128)S(1)}, u32[]{:S(2)}, u32[]{:S(2)}) async-start(s32[32,1,9]{2,1,0:T(1,128)} %bitcast.28), calls=%async_computation | async-start | bytes 32768 | tf_op jit(solution)/shard_map/all_to_all | solution.py:79
  27.8 21.6 %copy-start.3 = (bf16[100,1521]{1,0:T(8,128)(2,1)S(1)}, bf16[100,1521]{1,0:T(8,128)(2,1)}, u32[]{:S(2)}) copy-start(bf16[100,1521]{1,0:T(8,128)(2,1)} %param.20) | copy-start | bytes 912604
  27.8 21.6 %copy-start.5 = (f32[3,100]{1,0:T(4,128)S(1)}, f32[3,100]{1,0:T(4,128)}, u32[]{:S(2)}) copy-start(f32[3,100]{1,0:T(4,128)} %param.23) | copy-start | bytes 3604
  31.3 9.2 %copy-start.9 = (s32[288]{0:T(512)}, s32[288]{0:T(512)S(1)}, u32[]{:S(2)}) copy-start(s32[288]{0:T(512)S(1)} %reshape.473) | copy-start | bytes 3460
  33.8 13.2 %all-to-all-start.1 = ((bf16[32,9,128]{2,1,0:T(8,128)(2,1)}), bf16[32,9,128]{2,1,0:T(8,128)(2,1)S(1)}, u32[]{:S(2)}, u32[]{:S(2)}) async-start(bf16[32,9,128]{2,1,0:T(8,128)(2,1)} %select_select_fusion), calls=%async_computation.1 | async-start | bytes 262144 | tf_op jit(solution)/shard_map/all_to_all | solution.py:83
  40.5 314.1 %all-reduce.6.cloned.1.call-start = ((), (), s32[]{:S(2)}) async-start(), calls=%async_computation.3 | async-start | bytes 2097152 | tf_op jit(solution)/shard_map/psum | solution.py:8
  53.3 4.4 copy-start.2
  61.1 1.1 copy-start.1
  66.3 0.7 copy-start.4
  66.3 3.2 copy-start.10
  69.7 0.5 copy-start.11
  74.0 4.4 copy-start.2
  81.9 1.1 copy-start.1
  87.1 0.7 copy-start.4
  87.1 3.2 copy-start.10
  90.4 0.5 copy-start.11
  94.8 4.4 copy-start.2
  102.6 1.1 copy-start.1
  107.8 0.7 copy-start.4
  107.8 3.2 copy-start.10
  111.1 0.5 copy-start.11
  115.5 4.4 copy-start.2
  123.3 1.1 copy-start.1
  128.5 0.7 copy-start.4
  128.6 3.2 copy-start.10
  131.9 0.5 copy-start.11
  136.3 4.4 copy-start.2
  144.1 1.1 copy-start.1
  149.3 0.7 copy-start.4
  149.3 3.2 copy-start.10
  152.6 0.5 copy-start.11
  157.0 4.4 copy-start.2
  164.8 1.1 copy-start.1
  170.0 0.7 copy-start.4
  170.0 3.2 copy-start.10
  173.4 0.5 copy-start.11
  177.8 4.4 copy-start.2
  185.6 1.1 copy-start.1
  190.8 0.7 copy-start.4
  190.8 3.2 copy-start.10
  194.1 0.5 copy-start.11
  198.5 4.4 copy-start.2
  206.3 1.1 copy-start.1
  211.5 0.7 copy-start.4
  211.5 3.2 copy-start.10
  214.9 0.5 copy-start.11
  215.4 3.8 copy-start.7
  219.2 278.6 %all-reduce.8.cloned.1.call-start = ((), (), s32[]{:S(2)}) async-start(), calls=%async_computation.4 | async-start | bytes 2097152 | tf_op jit(solution)/shard_map/psum | solution.py:115
Sparse Core Ops, SparseCore 0:
  219.3 135.2 all-reduce.5
  356.9 140.7 all-reduce.7
